TPU v7x, 32 devices: a whole 2x2x4 slice. The times are simulated.
32 devices in a mesh: sub: 16 (over z, y, x), mode: 2 (over core).
Axes of the slice: x: 2, y: 2, z: 4, core: 2. Of those that a mesh axis runs over, the one named last changes fastest.
Arguments:
- coupling: bfloat16 [1024, 64, 128], P('sub'), may hold values from -0.5 to 0.5
- coupling_pairs: int32 [1024, 2], P('sub'), may hold values from 0 to 3, as said below
- modes: bfloat16 [1024, 256, 256], P('sub', None, 'mode'), may hold values from -6 to 6
- mode_weights: bfloat16 [1024, 256], P('sub', 'mode'), may hold values from 0 to 1, as said below
- parent_of: int32 [1024, 1], P('sub'), may hold values from 0 to 15; in each aligned block of 64 rows (0 to 63, 64 to 127, ...) at most 8 rows name the same one
- row_block: int32 [1024], P('sub'), may hold values from 0 to 7
- parent_modes: bfloat16 [16, 512, 256], P('sub'), may hold values from -1 to 1
- parent_eigs: float32 [16, 256], P('sub'), may hold values from 0.02 to 0.5
Outputs:
- strengths: float32 [1024, 256], P('sub', 'mode')
Inputs may be any that keep to these rules, and one draw needn't show every extreme that they name: `coupling_pairs`: within each child the 2 block indices are distinct. `parent_of`: the 64 children of one index of sub name any one parent at most 8 times; some parent is named exactly 8 times by some index's children. `mode_weights`: Positive.
All inputs are finite; a program needn't handle non-finite values.
Results may differ from a plain program's by a relative error of at most 0.0015.
Values may be sent and summed in bfloat16 or wider, within the bound.
A program may use at most 128 MiB of HBM per device.

v0:
```python
import jax
import jax.numpy as jnp
from jax import lax
from jax.sharding import PartitionSpec as P

M = 256
MP = 256
BLK = 64
CH_DEV = 64


def pick_blocks(modes, coupling_pairs):
    child_count, interface_rows, mode_cols = modes.shape
    blocks = modes.reshape(child_count, interface_rows // BLK, BLK, mode_cols)
    selector = (
        coupling_pairs[:, :, None]
        == jnp.arange(interface_rows // BLK, dtype=jnp.int32)[None, None, :]
    ).astype(jnp.bfloat16)
    picked = jnp.einsum(
        "skb,sbim->skim", selector, blocks, preferred_element_type=jnp.float32
    ).astype(jnp.bfloat16)
    return picked.reshape(child_count, coupling_pairs.shape[1] * BLK, mode_cols)


def weighted_records(coupling_rows, picked, weights):
    record = jnp.einsum("sij,sjm->sim", coupling_rows, picked, preferred_element_type=jnp.float32)
    return (record * weights[:, None, :].astype(jnp.float32)).astype(jnp.bfloat16)


def to_slots(values, slot_index, slot_count):
    empty = jnp.zeros((slot_count,) + values.shape[1:], values.dtype)
    return empty.at[slot_index].set(values)


def per_device(
    coupling, coupling_pairs, modes, mode_weights, parent_of, row_block, parent_modes, parent_eigs
):
    sub_count = lax.axis_size("sub")
    child_count = coupling.shape[0]
    mode_cols = modes.shape[2]
    capacity = max(2, 2 * child_count // sub_count)
    slot_count = sub_count * capacity
    owner = parent_of[:, 0]
    order_ids = jnp.arange(child_count, dtype=jnp.int32)
    earlier = (owner[:, None] == owner[None, :]) & (order_ids[None, :] < order_ids[:, None])
    position = jnp.sum(earlier.astype(jnp.int32), axis=1)
    slot_index = owner * capacity + position
    picked = pick_blocks(modes, coupling_pairs)
    row_send = to_slots(row_block, slot_index, slot_count).reshape(sub_count, capacity)
    record = weighted_records(coupling, picked, mode_weights)
    record_send = to_slots(record, slot_index, slot_count).reshape(
        sub_count, capacity, BLK, mode_cols
    )
    record_recv, row_recv = (
        lax.all_to_all(record_send, "sub", split_axis=0, concat_axis=0, tiled=True),
        lax.all_to_all(row_send, "sub", split_axis=0, concat_axis=0, tiled=True),
    )
    records = record_recv.reshape(slot_count, BLK, mode_cols)
    row_index = row_recv.reshape(slot_count)
    sep_blocks = parent_modes.shape[1] // BLK
    parent_blocks = parent_modes[0].reshape(sep_blocks, BLK, MP)
    group_size = min(64, slot_count)
    group_count = slot_count // group_size
    record_groups = records.reshape(group_count, group_size, BLK, mode_cols)
    row_groups = row_index.reshape(group_count, group_size)

    def project(gram_sum, members):
        record_part, row_part = members
        selector = (row_part[:, None] == jnp.arange(sep_blocks, dtype=jnp.int32)[None, :]).astype(
            jnp.bfloat16
        )
        parent_rows = jnp.einsum(
            "sb,bik->sik", selector, parent_blocks, preferred_element_type=jnp.float32
        ).astype(jnp.bfloat16)
        projected = jnp.einsum(
            "sik,sim->skm", parent_rows, record_part, preferred_element_type=jnp.float32
        ).astype(jnp.bfloat16)
        term = jnp.einsum("skm,slm->kl", projected, projected, preferred_element_type=jnp.float32)
        return (gram_sum + term, projected)

    gram_sum, projected_all = lax.scan(
        project, jnp.zeros((MP, MP), jnp.float32), (record_groups, row_groups)
    )
    gram_sum = lax.psum(gram_sum, "mode")
    pencil = jnp.diag(parent_eigs[0]) + gram_sum / (CH_DEV * M)
    factor = jnp.linalg.cholesky(pencil)
    identity = jnp.eye(MP, dtype=pencil.dtype)
    inverse = lax.linalg.triangular_solve(factor, identity, left_side=True, lower=True).astype(
        jnp.bfloat16
    )

    def strength(projected):
        rotated = jnp.einsum("kl,slm->skm", inverse, projected, preferred_element_type=jnp.float32)
        return jnp.sum(rotated * rotated, axis=1) / MP

    slot_values = lax.map(strength, projected_all).reshape(sub_count, capacity, mode_cols)
    returned = lax.all_to_all(slot_values, "sub", split_axis=0, concat_axis=0, tiled=True)
    return returned.reshape(slot_count, mode_cols)[slot_index]


def solution(mesh):
    in_specs = (
        P("sub", None, None),
        P("sub", None),
        P("sub", None, "mode"),
        P("sub", "mode"),
        P("sub", None),
        P("sub"),
        P("sub", None, None),
        P("sub", None),
    )
    out_specs = P("sub", "mode")
    return jax.shard_map(
        per_device, mesh=mesh, in_specs=in_specs, out_specs=out_specs, check_vma=False
    )
```

profile of v0, /device:TPU:0, one launch (start us, length us, event | category | flops | bytes accessed | tf_op | source)
XLA Modules:
  0.0 229.0 jit_solution(5430570650498612388)
XLA Ops:
  6.5 0.9 convert_reduce_fusion
  7.5 0.7 fusion.31
  8.1 0.9 scatter_custom_fusion
  9.1 0.7 all_to_all.12
  9.7 8.3 %all-to-all-start = ((s32[16,1,8]{2,1,0:T(1,128)}), s32[16,1,8]{2,1,0:T(1,128)S(1)}, u32[]{:S(2)}, u32[]{:S(2)}) async-start(s32[16,1,8]{2,1,0:T(1,128)} %bitcast.6), calls=%async_computation | async-start | bytes 16384 | tf_op jit(solution)/shard_map/all_to_all | solution.py:56
  18.1 0.8 copy.57
  18.9 5.6 %fusion.15 = bf16[64,2,64,128]{3,1,2,0:T(2,128)(2,1)S(1)} fusion(bf16[64,4,64,128]{3,2,1,0:T(8,128)(2,1)} %bitcast.113, s32[64,2]{1,0:T(8,128)S(1)} %copy.57), kind=kOutput, calls=%fused_computation.27 | convolution fusion | flops 9437696 | bytes 6291968 | tf_op jit(solution)/shard_map/skb,sbim->skim/dot_general | solution.py:19
  24.5 0.6 copy.59
  25.2 1.7 fusion.18
  26.9 0.5 broadcast_in_dim.55
  27.4 6.2 %scatter_fusion = bf16[128,64,128]{2,1,0:T(8,128)(2,1)S(1)} fusion(bf16[128,64,128]{2,1,0:T(8,128)(2,1)S(1)} %broadcast_in_dim.55, s32[64]{0:T(128)S(1)} %fusion.31, bf16[64,64,128]{2,1,0:T(8,128)(2,1)} %fusion.18), kind=kCustom, calls=%fused_computation.2 | custom fusion | bytes 3145984 | tf_op jit(solution)/shard_map/scatter | solution.py:32
  33.6 1.4 copy-done.1
  35.0 6.9 %all-to-all-start.1 = ((bf16[16,8,64,128]{3,2,1,0:T(8,128)(2,1)}), bf16[16,8,64,128]{3,2,1,0:T(8,128)(2,1)S(1)}, u32[]{:S(2)}, u32[]{:S(2)}) async-start(bf16[16,8,64,128]{3,2,1,0:T(8,128)(2,1)} %bitcast.107), calls=%async_computation.1 | async-start | bytes 4194304 | tf_op jit(solution)/shard_map/all_to_all | solution.py:55
  42.0 1.1 copy.60
  43.1 0.6 broadcast.151
  43.6 0.7 reduce.16
  44.4 40.2 %all-to-all-done.1 = bf16[16,8,64,128]{3,2,1,0:T(8,128)(2,1)S(1)} async-done(((bf16[16,8,64,128]{3,2,1,0:T(8,128)(2,1)}), bf16[16,8,64,128]{3,2,1,0:T(8,128)(2,1)S(1)}, u32[]{:S(2)}, u32[]{:S(2)}) %all-to-all-start.1) | async-done | bytes 2097184 | tf_op jit(solution)/shard_map/all_to_all | solution.py:55
  84.6 24.0 %while.26 = (s32[]{:T(128)}, f32[256,256]{1,0:T(8,128)}, bf16[2,64,256,128]{3,2,1,0:T(8,128)(2,1)}, s32[2,64]{1,0:T(2,128)S(1)}, bf16[8,64,256]{2,0,1:T(8,128)(2...) while((s32[]{:T(128)}, f32[256,256]{1,0:T(8,128)}, ...), condition=%wide.region_4.5_spmd.clone, body=%wide.region_3.4_spmd.clone.sunk | while | flops 1362231808 | bytes 18614116 | solution.py:81
  84.6 0.7 convolution_convert_fusion.4
  85.4 5.7 %bitcast_dynamic-update-slice_fusion.8 = (bf16[2,64,256,128]{3,2,1,0:T(8,128)(2,1)}, bf16[64,256,128]{2,1,0:T(8,128)(2,1)}) fusion(bf16[2,64,256,128]{3,2,1,0:T(8,128)(2,1)} %get-tuple-element.287, s32[]{:T(128)} %get-tuple-element.285, bf16[2,64,64,128]{3,2,1,0:T(8,128)(2,1)S(1)} %get-tuple-element.298, ...), kind=kOutput, calls=%fused_computation.11.clone.1 | convolution fusion | flops 270532608 | bytes 11535360 | tf_op jit(solution)/shard_map/while/body/eval_jaxpr/sik,sim->skm/dot_general | solution.py:75
  91.1 5.5 %fusion.62 = f32[256,256]{1,0:T(8,128)} fusion(bf16[64,256,128]{2,1,0:T(8,128)(2,1)} %get-tuple-element.275, f32[256,256]{1,0:T(8,128)} %get-tuple-element.286, pred[]{:T(512)S(6)} %compare.26), kind=kOutput, calls=%fused_computation.16.clone.1 | convolution fusion | flops 1073872896 | bytes 4718593 | tf_op jit(solution)/shard_map/while/body/eval_jaxpr/skm,slm->kl/dot_general | solution.py:78
  96.6 0.8 convolution_convert_fusion.4
  97.3 5.8 %bitcast_dynamic-update-slice_fusion.8 = (bf16[2,64,256,128]{3,2,1,0:T(8,128)(2,1)}, bf16[64,256,128]{2,1,0:T(8,128)(2,1)}) fusion(bf16[2,64,256,128]{3,2,1,0:T(8,128)(2,1)} %get-tuple-element.287, s32[]{:T(128)} %get-tuple-element.285, bf16[2,64,64,128]{3,2,1,0:T(8,128)(2,1)S(1)} %get-tuple-element.298, ...), kind=kOutput, calls=%fused_computation.11.clone.1 | convolution fusion | flops 270532608 | bytes 11535360 | tf_op jit(solution)/shard_map/while/body/eval_jaxpr/sik,sim->skm/dot_general | solution.py:75
  103.1 5.5 %fusion.62 = f32[256,256]{1,0:T(8,128)} fusion(bf16[64,256,128]{2,1,0:T(8,128)(2,1)} %get-tuple-element.275, f32[256,256]{1,0:T(8,128)} %get-tuple-element.286, pred[]{:T(512)S(6)} %compare.26), kind=kOutput, calls=%fused_computation.16.clone.1 | convolution fusion | flops 1073872896 | bytes 4718593 | tf_op jit(solution)/shard_map/while/body/eval_jaxpr/skm,slm->kl/dot_general | solution.py:78
  108.6 1.8 copy.61
  110.5 22.5 %all-reduce.3.cloned.1.call-done = f32[256,256]{0,1:T(8,128)} async-done(((f32[256,256]{0,1:T(8,128)}), f32[256,256]{0,1:T(8,128)}) %all-reduce.3.cloned.1.call-update) | async-done | bytes 262160 | tf_op jit(solution)/shard_map/psum | solution.py:84
  133.0 1.0 multiply_add_fusion
  134.1 1.0 fusion.19
  135.2 11.7 %cholesky.49 = f32[128,128]{1,0:T(8,128)S(1)} custom-call(f32[128,128]{1,0:T(8,128)S(1)} %cholesky.115), custom_call_target="Cholesky" | custom-call | tf_op jit(solution)/shard_map/jit(cholesky)/cholesky | solution.py:86
  146.9 9.8 %custom-call.14 = f32[1,128,128]{1,2,0:T(8,128)S(1)} custom-call(f32[1,128,128]{2,1,0:T(8,128)S(1)} %get-tuple-element.177), custom_call_target="InvertDiagBlocksLowerTriangular" | custom-call | tf_op jit(solution)/shard_map/jit(cholesky)/cholesky | solution.py:86
  157.2 11.7 %cholesky.103 = f32[128,128]{1,0:T(8,128)S(1)} custom-call(f32[128,128]{1,0:T(8,128)S(1)} %convolution_subtract_fusion.1), custom_call_target="Cholesky" | custom-call | tf_op jit(solution)/shard_map/jit(cholesky)/cholesky | solution.py:86
  169.3 0.7 compare_reduce_fusion
  171.3 4.0 %while.25 = (s32[]{:T(128)}, f32[256,256]{0,1:T(8,128)S(1)}, s32[2,2]{1,0:T(2,128)S(1)}, f32[2,128,128]{2,1,0:T(8,128)S(1)}, s32[]{:T(128)}) while((s32[]{:T(128)}, f32[256,256]{0,1:T(8,128)S(1)}, s32[2,2]{1,0:T(2,128)S(1)}, f32[2,128,128]{2,1,0:T(8,128)S(1)}, s32[]{:T(128)}) %tuple.70), condition=%wide.while_cond, body=%wide.while_body.sunk | while | flops 2 | bytes 393321 | solution.py:88
  171.3 0.6 fusion.56
  171.8 1.3 dynamic-slice.7
  173.3 0.6 fusion.56
  173.8 1.3 dynamic-slice.7
  175.3 19.9 %custom-call.15 = f32[2,128,128]{1,2,0:T(8,128)S(1)} custom-call(f32[2,128,128]{2,1,0:T(8,128)S(1)} %get-tuple-element.70), custom_call_target="InvertDiagBlocksLowerTriangular" | custom-call | tf_op jit(solution)/shard_map/triangular_solve | solution.py:88
  195.4 0.4 convolution_subtract_fusion
  195.8 0.3 convolution_convert_fusion.2
  196.2 10.5 %while.24 = (s32[]{:T(128)}, f32[2,64,128]{2,1,0:T(8,128)}, bf16[2,64,256,128]{3,2,1,0:T(8,128)(2,1)}, bf16[256,256]{1,0:T(8,128)(2,1)S(1)}, s32[]{:T(128)}) while((s32[]{:T(128)}, f32[2,64,128]{2,1,0:T(8,128)}, bf16[2,64,256,128]{3,2,1,0:T(8,128)(2,1)}, bf16[256,256]{1,0:T(8,128)(2,1)S(1)}, s32[]{:T(128)}) %tuple.73), condition=%wide.region_12.13_spmd, body=%wide.region_10.12_spmd.sunk | while | flops 1077936128 | bytes 4424765 | solution.py:96
  196.2 4.6 %multiply_reduce_fusion.2 = f32[64,128]{1,0:T(8,128)S(1)} fusion(bf16[2,64,256,128]{3,2,1,0:T(8,128)(2,1)} %get-tuple-element.328, s32[]{:T(128)} %get-tuple-element.321, bf16[256,256]{1,0:T(8,128)(2,1)S(1)} %get-tuple-element.329), kind=kOutput, calls=%fused_computation.3.clone.1 | convolution fusion | flops 1077927936 | bytes 4358656 | tf_op jit(solution)/shard_map/while/body/eval_jaxpr/kl,slm->skm/dot_general | solution.py:93
  200.8 0.6 bitcast_dynamic-update-slice_fusion.6
  201.4 4.6 %multiply_reduce_fusion.2 = f32[64,128]{1,0:T(8,128)S(1)} fusion(bf16[2,64,256,128]{3,2,1,0:T(8,128)(2,1)} %get-tuple-element.328, s32[]{:T(128)} %get-tuple-element.321, bf16[256,256]{1,0:T(8,128)(2,1)S(1)} %get-tuple-element.329), kind=kOutput, calls=%fused_computation.3.clone.1 | convolution fusion | flops 1077927936 | bytes 4358656 | tf_op jit(solution)/shard_map/while/body/eval_jaxpr/kl,slm->skm/dot_general | solution.py:93
  206.0 0.6 bitcast_dynamic-update-slice_fusion.6
  206.6 6.8 %all-to-all-start.2 = ((f32[16,8,128]{2,1,0:T(8,128)}), f32[16,8,128]{2,1,0:T(8,128)S(1)}, u32[]{:S(2)}, u32[]{:S(2)}) async-start(f32[16,8,128]{2,1,0:T(8,128)} %bitcast.21), calls=%async_computation.2 | async-start | bytes 131072 | tf_op jit(solution)/shard_map/all_to_all | solution.py:97
  213.5 7.5 %all-to-all-done.2 = f32[16,8,128]{2,1,0:T(8,128)S(1)} async-done(((f32[16,8,128]{2,1,0:T(8,128)}), f32[16,8,128]{2,1,0:T(8,128)S(1)}, u32[]{:S(2)}, u32[]{:S(2)}) %all-to-all-start.2) | async-done | bytes 65568 | tf_op jit(solution)/shard_map/all_to_all | solution.py:97
  221.0 1.2 gather_fusion
  (43 shorter events, 1.9 us)
Async XLA Ops:
  6.5 18.6 %copy-start = (bf16[64,64,128]{2,1,0:T(8,128)(2,1)S(1)}, bf16[64,64,128]{2,1,0:T(8,128)(2,1)}, u32[]{:S(2)}) copy-start(bf16[64,64,128]{2,1,0:T(8,128)(2,1)} %param.12) | copy-start | bytes 3145732
  9.7 23.8 %all-to-all-start = ((s32[16,1,8]{2,1,0:T(1,128)}), s32[16,1,8]{2,1,0:T(1,128)S(1)}, u32[]{:S(2)}, u32[]{:S(2)}) async-start(s32[16,1,8]{2,1,0:T(1,128)} %bitcast.6), calls=%async_computation | async-start | bytes 16384 | tf_op jit(solution)/shard_map/all_to_all | solution.py:56
  24.5 0.7 copy-start.2
  33.6 1.4 copy-start.1
  35.0 49.6 %all-to-all-start.1 = ((bf16[16,8,64,128]{3,2,1,0:T(8,128)(2,1)}), bf16[16,8,64,128]{3,2,1,0:T(8,128)(2,1)S(1)}, u32[]{:S(2)}, u32[]{:S(2)}) async-start(bf16[16,8,64,128]{3,2,1,0:T(8,128)(2,1)} %bitcast.107), calls=%async_computation.1 | async-start | bytes 4194304 | tf_op jit(solution)/shard_map/all_to_all | solution.py:55
  41.9 91.1 %all-reduce.3.cloned.1.call-start = ((), (), s32[]{:S(2)}) async-start(), calls=%async_computation.3 | async-start | bytes 524288 | tf_op jit(solution)/shard_map/psum | solution.py:84
  84.6 48.4 %copy-start.3 = (f32[1,256]{1,0:T(1,128)S(1)}, f32[1,256]{1,0:T(1,128)}, u32[]{:S(2)}) copy-start(f32[1,256]{1,0:T(1,128)} %param.19) | copy-start | bytes 3076
  206.6 14.4 %all-to-all-start.2 = ((f32[16,8,128]{2,1,0:T(8,128)}), f32[16,8,128]{2,1,0:T(8,128)S(1)}, u32[]{:S(2)}, u32[]{:S(2)}) async-start(f32[16,8,128]{2,1,0:T(8,128)} %bitcast.21), calls=%async_computation.2 | async-start | bytes 131072 | tf_op jit(solution)/shard_map/all_to_all | solution.py:97
Sparse Core Ops, SparseCore 0:
  110.5 22.4 all-reduce.2
where the time goes:
time: 230 us; the launch traced here: 229 us
  waiting for transfers between devices  70.3 us (31%)
  other arithmetic  59.4 us (26%)
  matrix products  41.9 us (18%)
  starting transfers between devices  22.1 us (10%)
  local copies, waits for them, and re-layouts  20.3 us (9%)
  between operations  14.9 us (6%)
    all_to_all x1, waiting for transfers between devices, per_device(): lax.all_to_all(record_send, 'sub', split_axis=0, concat_axis=0, tiled=True)  40.2 us
    another operation x6, other arithmetic, per_device(): factor = jnp.linalg.cholesky(pencil)  34 us
    psum x1, waiting for transfers between devices, per_device(): gram_sum = lax.psum(gram_sum, 'mode')  22.5 us
    another operation x4, other arithmetic, per_device(): lax.linalg.triangular_solve(factor, identity, left_side=True, lower=True)  19.9 us
    dot_general x2, matrix products, project(): jnp.einsum('sik,sim->skm', parent_rows, record_part, preferred_element_ty...  11.5 us
    dot_general x2, matrix products, project(): jnp.einsum('skm,slm->kl', projected, projected, preferred_element_type=jn...  11 us
    dot_general x2, matrix products, strength(): jnp.einsum('kl,slm->skm', inverse, projected, preferred_element_type=jnp....  9.22 us
    all_to_all x1, starting transfers between devices, per_device(): lax.all_to_all(row_send, 'sub', split_axis=0, concat_axis=0, tiled=True)  8.34 us
  transfers between devices with their start and end apart: 4, of which 3 were waited for; matrix products, arithmetic and copies ran while one was open for 8% of the time, Pallas kernels for 0%

commit v1 on v0

--- a/solution.py
+++ b/solution.py
@@ -81,7 +81,7 @@
     gram_sum, projected_all = lax.scan(
         project, jnp.zeros((MP, MP), jnp.float32), (record_groups, row_groups)
     )
-    gram_sum = lax.psum(gram_sum, "mode")
+    gram_sum = jnp.sum(lax.all_gather(gram_sum, "mode"), axis=0)
     pencil = jnp.diag(parent_eigs[0]) + gram_sum / (CH_DEV * M)
     factor = jnp.linalg.cholesky(pencil)
     identity = jnp.eye(MP, dtype=pencil.dtype)

time: 230 us -> 198 us (0.86)
  waiting for transfers between devices: 70.3 us -> 47.7 us
  between operations: 14.9 us -> 1.55 us
  starting transfers between devices: 22.1 us -> 25.1 us
  blocking collectives: 0 us -> 2.56 us
    psum x1 -> x0, waiting for transfers between devices: 22.5 us -> none  [per_device(): gram_sum = lax.psum(gram_sum, 'mode')]
    all_to_all x1, starting transfers between devices: 6.83 us -> 9.83 us  [per_device(): lax.all_to_all(slot_values, 'sub', split_axis=0, concat_axis=0, tiled=True)]
    all_gather x0 -> x1, blocking collectives: none -> 2.56 us  [per_device(): gram_sum = jnp.sum(lax.all_gather(gram_sum, 'mode'), axis=0)]
  transfers between devices with their start and end apart: 4 -> 3, of which waited for: 3 -> 2; matrix products, arithmetic and copies ran while one was open for 8% -> 9% of each run, Pallas kernels for 0% -> 0%
where the time goes in v1:
time: 198 us; the launch traced here: 197 us
  other arithmetic  58.2 us (29%)
  waiting for transfers between devices  47.7 us (24%)
  matrix products  41.9 us (21%)
  starting transfers between devices  25.1 us (13%)
  local copies, waits for them, and re-layouts  20.1 us (10%)
  blocking collectives  2.56 us (1%)
    all_to_all x1, waiting for transfers between devices, per_device(): lax.all_to_all(record_send, 'sub', split_axis=0, concat_axis=0, tiled=True)  40.2 us
    another operation x6, other arithmetic, per_device(): factor = jnp.linalg.cholesky(pencil)  33.9 us
    another operation x4, other arithmetic, per_device(): lax.linalg.triangular_solve(factor, identity, left_side=True, lower=True)  20.5 us
    dot_general x2, matrix products, project(): jnp.einsum('sik,sim->skm', parent_rows, record_part, preferred_element_ty...  11.5 us
    dot_general x2, matrix products, project(): jnp.einsum('skm,slm->kl', projected, projected, preferred_element_type=jn...  11 us
    all_to_all x1, starting transfers between devices, per_device(): lax.all_to_all(slot_values, 'sub', split_axis=0, concat_axis=0, tiled=True)  9.83 us
    dot_general x2, matrix products, strength(): jnp.einsum('kl,slm->skm', inverse, projected, preferred_element_type=jnp....  9.22 us
    all_to_all x1, starting transfers between devices, per_device(): lax.all_to_all(row_send, 'sub', split_axis=0, concat_axis=0, tiled=True)  8.34 us
  transfers between devices with their start and end apart: 3, of which 2 were waited for; matrix products, arithmetic and copies ran while one was open for 9% of the time, Pallas kernels for 0%

profile of v1, /device:TPU:0, one launch (start us, length us, event | category | flops | bytes accessed | tf_op | source)
XLA Modules:
  0.0 197.4 jit_solution(18015423203249322042)
XLA Ops:
  0.0 0.9 convert_reduce_fusion
  0.9 0.7 fusion.33
  1.6 0.9 scatter_custom_fusion
  2.5 0.7 all_to_all.12
  3.2 8.3 %all-to-all-start = ((s32[16,1,8]{2,1,0:T(1,128)}), s32[16,1,8]{2,1,0:T(1,128)S(1)}, u32[]{:S(2)}, u32[]{:S(2)}) async-start(s32[16,1,8]{2,1,0:T(1,128)} %bitcast.6), calls=%async_computation | async-start | bytes 16384 | tf_op jit(solution)/shard_map/all_to_all | solution.py:56
  11.6 0.8 copy.59
  12.3 5.6 %fusion.15 = bf16[64,2,64,128]{3,1,2,0:T(2,128)(2,1)S(1)} fusion(bf16[64,4,64,128]{3,2,1,0:T(8,128)(2,1)} %bitcast.116, s32[64,2]{1,0:T(8,128)S(1)} %copy.59), kind=kOutput, calls=%fused_computation.27 | convolution fusion | flops 9437696 | bytes 6291968 | tf_op jit(solution)/shard_map/skb,sbim->skim/dot_general | solution.py:19
  17.9 0.6 copy.61
  18.6 1.7 fusion.18
  20.3 0.5 broadcast_in_dim.57
  20.9 6.2 %scatter_fusion = bf16[128,64,128]{2,1,0:T(8,128)(2,1)S(1)} fusion(bf16[128,64,128]{2,1,0:T(8,128)(2,1)S(1)} %broadcast_in_dim.57, s32[64]{0:T(128)S(1)} %fusion.33, bf16[64,64,128]{2,1,0:T(8,128)(2,1)} %fusion.18), kind=kCustom, calls=%fused_computation.2 | custom fusion | bytes 3145984 | tf_op jit(solution)/shard_map/scatter | solution.py:32
  27.1 1.4 copy-done.1
  28.4 6.9 %all-to-all-start.1 = ((bf16[16,8,64,128]{3,2,1,0:T(8,128)(2,1)}), bf16[16,8,64,128]{3,2,1,0:T(8,128)(2,1)S(1)}, u32[]{:S(2)}, u32[]{:S(2)}) async-start(bf16[16,8,64,128]{3,2,1,0:T(8,128)(2,1)} %bitcast.110), calls=%async_computation.1 | async-start | bytes 4194304 | tf_op jit(solution)/shard_map/all_to_all | solution.py:55
  35.4 1.1 copy.62
  36.5 0.6 broadcast.156
  37.1 0.7 reduce.16
  37.9 40.2 %all-to-all-done.1 = bf16[16,8,64,128]{3,2,1,0:T(8,128)(2,1)S(1)} async-done(((bf16[16,8,64,128]{3,2,1,0:T(8,128)(2,1)}), bf16[16,8,64,128]{3,2,1,0:T(8,128)(2,1)S(1)}, u32[]{:S(2)}, u32[]{:S(2)}) %all-to-all-start.1) | async-done | bytes 2097184 | tf_op jit(solution)/shard_map/all_to_all | solution.py:55
  78.1 24.0 %while.26 = (s32[]{:T(128)}, f32[256,256]{1,0:T(8,128)}, bf16[2,64,256,128]{3,2,1,0:T(8,128)(2,1)}, s32[2,64]{1,0:T(2,128)S(1)}, bf16[8,64,256]{2,0,1:T(8,128)(2...) while((s32[]{:T(128)}, f32[256,256]{1,0:T(8,128)}, ...), condition=%wide.region_4.5_spmd.clone, body=%wide.region_3.4_spmd.clone.sunk | while | flops 1362231808 | bytes 18614116 | solution.py:81
  78.1 0.7 convolution_convert_fusion.4
  78.8 5.7 %bitcast_dynamic-update-slice_fusion.8 = (bf16[2,64,256,128]{3,2,1,0:T(8,128)(2,1)}, bf16[64,256,128]{2,1,0:T(8,128)(2,1)}) fusion(bf16[2,64,256,128]{3,2,1,0:T(8,128)(2,1)} %get-tuple-element.289, s32[]{:T(128)} %get-tuple-element.287, bf16[2,64,64,128]{3,2,1,0:T(8,128)(2,1)S(1)} %get-tuple-element.300, ...), kind=kOutput, calls=%fused_computation.11.clone.1 | convolution fusion | flops 270532608 | bytes 11535360 | tf_op jit(solution)/shard_map/while/body/eval_jaxpr/sik,sim->skm/dot_general | solution.py:75
  84.6 5.5 %fusion.64 = f32[256,256]{1,0:T(8,128)} fusion(bf16[64,256,128]{2,1,0:T(8,128)(2,1)} %get-tuple-element.277, f32[256,256]{1,0:T(8,128)} %get-tuple-element.288, pred[]{:T(512)S(6)} %compare.26), kind=kOutput, calls=%fused_computation.16.clone.1 | convolution fusion | flops 1073872896 | bytes 4718593 | tf_op jit(solution)/shard_map/while/body/eval_jaxpr/skm,slm->kl/dot_general | solution.py:78
  90.0 0.8 convolution_convert_fusion.4
  90.8 5.8 %bitcast_dynamic-update-slice_fusion.8 = (bf16[2,64,256,128]{3,2,1,0:T(8,128)(2,1)}, bf16[64,256,128]{2,1,0:T(8,128)(2,1)}) fusion(bf16[2,64,256,128]{3,2,1,0:T(8,128)(2,1)} %get-tuple-element.289, s32[]{:T(128)} %get-tuple-element.287, bf16[2,64,64,128]{3,2,1,0:T(8,128)(2,1)S(1)} %get-tuple-element.300, ...), kind=kOutput, calls=%fused_computation.11.clone.1 | convolution fusion | flops 270532608 | bytes 11535360 | tf_op jit(solution)/shard_map/while/body/eval_jaxpr/sik,sim->skm/dot_general | solution.py:75
  96.6 5.5 %fusion.64 = f32[256,256]{1,0:T(8,128)} fusion(bf16[64,256,128]{2,1,0:T(8,128)(2,1)} %get-tuple-element.277, f32[256,256]{1,0:T(8,128)} %get-tuple-element.288, pred[]{:T(512)S(6)} %compare.26), kind=kOutput, calls=%fused_computation.16.clone.1 | convolution fusion | flops 1073872896 | bytes 4718593 | tf_op jit(solution)/shard_map/while/body/eval_jaxpr/skm,slm->kl/dot_general | solution.py:78
  102.1 2.6 %all-gather = f32[512,256]{1,0:T(8,128)S(1)} all-gather(f32[256,256]{1,0:T(8,128)} %get-tuple-element.61), channel_id=2, replica_groups=mesh['sub'=16,'mode'=2] {'mode'}, dimensions={0}, use_global_device_ids=true | all-gather | bytes 786432 | tf_op jit(solution)/shard_map/all_gather | solution.py:84
  105.3 11.7 %cholesky.49 = f32[128,128]{1,0:T(8,128)S(1)} custom-call(f32[128,128]{1,0:T(8,128)S(1)} %cholesky.115), custom_call_target="Cholesky" | custom-call | tf_op jit(solution)/shard_map/jit(cholesky)/cholesky | solution.py:86
  117.0 9.8 %custom-call.14 = f32[1,128,128]{1,2,0:T(8,128)S(1)} custom-call(f32[1,128,128]{2,1,0:T(8,128)S(1)} %get-tuple-element.177), custom_call_target="InvertDiagBlocksLowerTriangular" | custom-call | tf_op jit(solution)/shard_map/jit(cholesky)/cholesky | solution.py:86
  127.0 0.3 convolution_subtract_fusion.1
  127.3 11.7 %cholesky.103 = f32[128,128]{1,0:T(8,128)S(1)} custom-call(f32[128,128]{1,0:T(8,128)S(1)} %convolution_subtract_fusion.1), custom_call_target="Cholesky" | custom-call | tf_op jit(solution)/shard_map/jit(cholesky)/cholesky | solution.py:86
  139.4 0.6 compare_reduce_fusion
  141.4 5.4 %while.25 = (s32[]{:T(128)}, f32[256,256]{0,1:T(8,128)S(1)}, s32[2,2]{1,0:T(2,128)S(1)}, f32[2,128,128]{2,1,0:T(8,128)}, s32[]{:T(128)}) while((s32[]{:T(128)}, f32[256,256]{0,1:T(8,128)S(1)}, s32[2,2]{1,0:T(2,128)S(1)}, f32[2,128,128]{2,1,0:T(8,128)}, s32[]{:T(128)}) %tuple.71), condition=%wide.while_cond, body=%wide.while_body.sunk | while | flops 2 | bytes 393829 | solution.py:88
  141.6 0.6 fusion.58
  142.2 1.3 dynamic-slice.7
  143.6 0.6 bitcast_dynamic-update-slice_fusion.7
  144.2 0.6 fusion.58
  144.8 1.3 dynamic-slice.7
  146.2 0.6 bitcast_dynamic-update-slice_fusion.7
  146.8 20.5 %custom-call.15 = f32[2,128,128]{1,2,0:T(8,128)S(1)} custom-call(f32[2,128,128]{2,1,0:T(8,128)} %get-tuple-element.70), custom_call_target="InvertDiagBlocksLowerTriangular" | custom-call | tf_op jit(solution)/shard_map/triangular_solve | solution.py:88
  167.6 0.4 convolution_subtract_fusion
  168.0 0.3 convolution_convert_fusion.2
  168.3 10.5 %while.24 = (s32[]{:T(128)}, f32[2,64,128]{2,1,0:T(8,128)}, bf16[2,64,256,128]{3,2,1,0:T(8,128)(2,1)}, bf16[256,256]{1,0:T(8,128)(2,1)S(1)}, s32[]{:T(128)}) while((s32[]{:T(128)}, f32[2,64,128]{2,1,0:T(8,128)}, bf16[2,64,256,128]{3,2,1,0:T(8,128)(2,1)}, bf16[256,256]{1,0:T(8,128)(2,1)S(1)}, s32[]{:T(128)}) %tuple.74), condition=%wide.region_12.13_spmd, body=%wide.region_10.12_spmd.sunk | while | flops 1077936128 | bytes 4424765 | solution.py:96
  168.3 4.6 %multiply_reduce_fusion.2 = f32[64,128]{1,0:T(8,128)S(1)} fusion(bf16[2,64,256,128]{3,2,1,0:T(8,128)(2,1)} %get-tuple-element.330, s32[]{:T(128)} %get-tuple-element.323, bf16[256,256]{1,0:T(8,128)(2,1)S(1)} %get-tuple-element.331), kind=kOutput, calls=%fused_computation.3.clone.1 | convolution fusion | flops 1077927936 | bytes 4358656 | tf_op jit(solution)/shard_map/while/body/eval_jaxpr/kl,slm->skm/dot_general | solution.py:93
  172.9 0.6 bitcast_dynamic-update-slice_fusion.6
  173.6 4.6 %multiply_reduce_fusion.2 = f32[64,128]{1,0:T(8,128)S(1)} fusion(bf16[2,64,256,128]{3,2,1,0:T(8,128)(2,1)} %get-tuple-element.330, s32[]{:T(128)} %get-tuple-element.323, bf16[256,256]{1,0:T(8,128)(2,1)S(1)} %get-tuple-element.331), kind=kOutput, calls=%fused_computation.3.clone.1 | convolution fusion | flops 1077927936 | bytes 4358656 | tf_op jit(solution)/shard_map/while/body/eval_jaxpr/kl,slm->skm/dot_general | solution.py:93
  178.2 0.6 bitcast_dynamic-update-slice_fusion.6
  178.8 9.8 %all-to-all-start.2 = ((f32[16,8,128]{2,1,0:T(8,128)}), f32[16,8,128]{2,1,0:T(8,128)S(1)}, u32[]{:S(2)}, u32[]{:S(2)}) async-start(f32[16,8,128]{2,1,0:T(8,128)} %bitcast.22), calls=%async_computation.2 | async-start | bytes 131072 | tf_op jit(solution)/shard_map/all_to_all | solution.py:97
  188.6 7.5 %all-to-all-done.2 = f32[16,8,128]{2,1,0:T(8,128)S(1)} async-done(((f32[16,8,128]{2,1,0:T(8,128)}), f32[16,8,128]{2,1,0:T(8,128)S(1)}, u32[]{:S(2)}, u32[]{:S(2)}) %all-to-all-start.2) | async-done | bytes 65568 | tf_op jit(solution)/shard_map/all_to_all | solution.py:97
  196.2 1.2 gather_fusion
  (43 shorter events, 2.0 us)
Async XLA Ops:
  0.0 18.6 %copy-start = (bf16[64,64,128]{2,1,0:T(8,128)(2,1)S(1)}, bf16[64,64,128]{2,1,0:T(8,128)(2,1)}, u32[]{:S(2)}) copy-start(bf16[64,64,128]{2,1,0:T(8,128)(2,1)} %param.12) | copy-start | bytes 3145732
  3.2 23.8 %all-to-all-start = ((s32[16,1,8]{2,1,0:T(1,128)}), s32[16,1,8]{2,1,0:T(1,128)S(1)}, u32[]{:S(2)}, u32[]{:S(2)}) async-start(s32[16,1,8]{2,1,0:T(1,128)} %bitcast.6), calls=%async_computation | async-start | bytes 16384 | tf_op jit(solution)/shard_map/all_to_all | solution.py:56
  17.9 0.7 copy-start.2
  27.0 1.4 copy-start.1
  28.4 49.6 %all-to-all-start.1 = ((bf16[16,8,64,128]{3,2,1,0:T(8,128)(2,1)}), bf16[16,8,64,128]{3,2,1,0:T(8,128)(2,1)S(1)}, u32[]{:S(2)}, u32[]{:S(2)}) async-start(bf16[16,8,64,128]{3,2,1,0:T(8,128)(2,1)} %bitcast.110), calls=%async_computation.1 | async-start | bytes 4194304 | tf_op jit(solution)/shard_map/all_to_all | solution.py:55
  78.1 26.7 %copy-start.3 = (f32[1,256]{1,0:T(1,128)S(1)}, f32[1,256]{1,0:T(1,128)}, u32[]{:S(2)}) copy-start(f32[1,256]{1,0:T(1,128)} %param.19) | copy-start | bytes 3076
  178.8 17.4 %all-to-all-start.2 = ((f32[16,8,128]{2,1,0:T(8,128)}), f32[16,8,128]{2,1,0:T(8,128)S(1)}, u32[]{:S(2)}, u32[]{:S(2)}) async-start(f32[16,8,128]{2,1,0:T(8,128)} %bitcast.22), calls=%async_computation.2 | async-start | bytes 131072 | tf_op jit(solution)/shard_map/all_to_all | solution.py:97
